TPU v7x, 128 devices: a whole 4x4x4 slice. The times are simulated.
128 devices in a mesh: row: 16 (over y, x), col: 8 (over z, core).
Axes of the slice: x: 4, y: 4, z: 4, core: 2. Of those that a mesh axis runs over, the one named last changes fastest.
Arguments:
- features: float32 [32768, 256], P(('row', 'col')), may hold values from -6 to 6
- loader_perm: int32 [32768], P(('row', 'col')), may hold values from 0 to 32767, as said below
- block_values: float32 [16, 8, 256, 4096], P('row', 'col'), may hold values from -0.09375 to 0.09375
- block_row: int32 [16, 8, 256], P('row', 'col'), may hold values from 0 to 63
- block_column: int32 [16, 8, 256], P('row', 'col'), may hold values from 0 to 31
- tile_count: int32 [16, 8], P('row', 'col'), may hold values from 32 to 256, as said below
- weight: float32 [256, 256], replicated, may hold values from -0.375 to 0.375
- bias_vector: float32 [256], replicated, may hold values from -0.5 to 0.5
- cotangent: float32 [32768, 256], P(('row', 'col')), may hold values from -6 to 6
Outputs:
- output: float32 [32768, 256], P(('row', 'col'))
- grad_x: float32 [32768, 256], P(('row', 'col'))
- grad_w: float32 [256, 256], replicated
- grad_b: float32 [256], replicated
Inputs may be any that keep to these rules, and one draw needn't show every extreme that they name: `loader_perm`: every grid position appears once; the 256 loader rows of any one device name the same number of positions, 256 divided by the number of devices, in each aligned block of 256 grid positions. `tile_count`: every count is 256 divided by 1, 2, 4 or 8; a block position may appear in several slots of a tile, and such blocks add.
All inputs are finite; a program needn't handle non-finite values.
Results may differ from a plain program's by a relative error of at most 0.0003.
Values sent between devices are 32-bit elements; how exact they have to be, the bound alone decides.
No kernel may reach another device: no remote copies, remote signals or barrier semaphores. Data moves between devices by JAX's collectives and lax.ppermute only.
A program may use at most 128 MiB of HBM per device.

v0:
```python
import math
import jax
import jax.numpy as jnp
from jax import lax
from jax.sharding import PartitionSpec as P

precise = lax.Precision.HIGHEST


def accumulate(
    accumulated,
    source_blocks,
    tile_vals,
    source_at,
    target_at,
    live_count,
    pattern,
    group_size,
    group_turns,
    block_size,
):

    def one_group(turn, partial_sum):
        first_slot = turn * group_size
        group_vals = lax.dynamic_slice_in_dim(tile_vals, first_slot, group_size, 0)
        from_at = lax.dynamic_slice_in_dim(source_at, first_slot, group_size, 0)
        into_at = lax.dynamic_slice_in_dim(target_at, first_slot, group_size, 0)
        alive = first_slot + jnp.arange(group_size, dtype=jnp.int32) < live_count
        group_vals = jnp.where(alive[:, None], group_vals, jnp.zeros_like(group_vals))
        group_vals = group_vals.reshape(group_size, block_size, block_size)
        terms = jnp.einsum(pattern, group_vals, source_blocks[from_at], precision=precise)
        return partial_sum.at[into_at].add(terms)

    return lax.fori_loop(0, group_turns, one_group, accumulated)


def on_device(
    features,
    loader_perm,
    block_values,
    block_row,
    block_column,
    tile_count,
    weight,
    bias_vector,
    cotangent,
):
    node_dev, feat_width = features.shape
    row_devices = lax.axis_size("row")
    col_devices = lax.axis_size("col")
    devices = row_devices * col_devices
    row_index = lax.axis_index("row")
    group_rows = col_devices * node_dev
    tile_vals = block_values[0, 0]
    tile_rows = block_row[0, 0]
    tile_columns = block_column[0, 0]
    live_count = tile_count[0, 0]
    block_size = math.isqrt(tile_vals.shape[-1])
    slot_total = tile_vals.shape[0]
    group_size = math.gcd(slot_total, 128)
    group_turns = slot_total // group_size
    per_group = node_dev // row_devices
    ordering = jnp.argsort(loader_perm // group_rows, stable=True)
    sent_rows = jnp.broadcast_to(
        features[ordering].reshape(row_devices, 1, per_group, feat_width),
        (row_devices, col_devices, per_group, feat_width),
    ).reshape(devices, per_group, feat_width)
    sent_ids = jnp.broadcast_to(
        loader_perm[ordering].astype(jnp.float32).reshape(row_devices, 1, per_group),
        (row_devices, col_devices, per_group),
    ).reshape(devices, per_group)
    got_rows, got_ids = (
        lax.all_to_all(sent_rows, ("row", "col"), split_axis=0, concat_axis=0, tiled=True),
        lax.all_to_all(sent_ids, ("row", "col"), split_axis=0, concat_axis=0, tiled=True),
    )
    local_pos = got_ids.reshape(group_rows).astype(jnp.int32) - row_index * group_rows
    panel_rows = got_rows.reshape(group_rows, feat_width)[jnp.argsort(local_pos)]
    out_blocks = row_devices * node_dev // block_size
    in_blocks = group_rows // block_size
    partial_value = accumulate(
        jnp.zeros((out_blocks, block_size, feat_width), jnp.float32),
        panel_rows.reshape(in_blocks, block_size, feat_width),
        tile_vals,
        tile_columns,
        tile_rows,
        live_count,
        "kab,kbf->kaf",
        group_size,
        group_turns,
        block_size,
    )
    partial_value = partial_value.reshape(row_devices * node_dev, feat_width)
    hidden = lax.psum_scatter(partial_value, "row", scatter_dimension=0, tiled=True)
    preact = jnp.dot(hidden, weight, precision=precise) + bias_vector
    squashed = jax.nn.sigmoid(preact)
    output = preact * squashed
    grad_pre = cotangent * squashed * (1.0 + preact * (1.0 - squashed))
    grad_hidden = jnp.dot(grad_pre, weight.T, precision=precise)
    column = lax.all_gather(grad_hidden, "row", axis=0, tiled=True)
    partial_x = accumulate(
        jnp.zeros((in_blocks, block_size, feat_width), jnp.float32),
        column.reshape(out_blocks, block_size, feat_width),
        tile_vals,
        tile_rows,
        tile_columns,
        live_count,
        "kba,kbf->kaf",
        group_size,
        group_turns,
        block_size,
    )
    grad_x = lax.psum_scatter(
        partial_x.reshape(group_rows, feat_width), "col", scatter_dimension=0, tiled=True
    )
    local_w = jnp.einsum("nf,ng->fg", hidden, grad_pre, precision=precise)
    local_b = jnp.sum(grad_pre, axis=0)
    grad_w, grad_b = lax.psum((local_w, local_b), ("row", "col"))
    norm_scale = 1.0 / math.sqrt(node_dev * devices)
    return (output, grad_x, grad_w * norm_scale, grad_b * norm_scale)


def solution(mesh):
    in_specs = (
        P(("row", "col"), None),
        P(("row", "col")),
        P("row", "col", None, None),
        P("row", "col", None),
        P("row", "col", None),
        P("row", "col"),
        P(),
        P(),
        P(("row", "col"), None),
    )
    out_specs = (P(("row", "col"), None), P(("row", "col"), None), P(), P())
    return jax.shard_map(
        on_device, mesh=mesh, in_specs=in_specs, out_specs=out_specs, check_vma=False
    )
```

profile of v0, /device:TPU:0, one launch (start us, length us, event | category | flops | bytes accessed | tf_op | source)
XLA Modules:
  0.0 511.8 jit_solution(5584946851250367723)
XLA Ops:
  7.9 3.2 sort.34
  13.8 11.2 %all-to-all-start.1 = ((f32[128,1,16]{2,1,0:T(1,128)}), f32[128,1,16]{2,1,0:T(1,128)S(1)}, u32[]{:S(2)}, u32[]{:S(2)}) async-start(f32[128,1,16]{2,1,0:T(1,128)} %bitcast.9), calls=%async_computation.1 | async-start | bytes 131072 | tf_op jit(solution)/shard_map/all_to_all | solution.py:74
  26.9 7.5 %all-to-all-done.1 = f32[128,1,16]{2,1,0:T(1,128)S(1)} async-done(((f32[128,1,16]{2,1,0:T(1,128)}), f32[128,1,16]{2,1,0:T(1,128)S(1)}, u32[]{:S(2)}, u32[]{:S(2)}) %all-to-all-start.1) | async-done | bytes 8224 | tf_op jit(solution)/shard_map/all_to_all | solution.py:74
  36.1 4.6 all-to-all-start
  40.8 5.6 %copy.19 = f32[1,1,256,4096]{2,3,1,0:T(8,128)} copy(f32[1,1,256,4096]{3,2,1,0:T(8,128)} %param.15) | data formatting | bytes 8388608 | tf_op args[2]
  46.7 5.0 sort.35
  51.7 19.4 %all-to-all-done = f32[128,16,256]{2,1,0:T(8,128)S(1)} async-done(((f32[128,16,256]{2,1,0:T(8,128)}), f32[128,16,256]{2,1,0:T(8,128)S(1)}, u32[]{:S(2)}, u32[]{:S(2)}) %all-to-all-start) | async-done | bytes 2097184 | tf_op jit(solution)/shard_map/all_to_all | solution.py:73
  72.5 8.2 %gather_fusion.4 = f32[2048,256]{1,0:T(8,128)S(1)} fusion(f32[2048,256]{1,0:T(8,128)} %bitcast.42, s32[2048]{0:T(1024)S(1)} %fusion.1), kind=kCustom, calls=%fused_computation.4 | custom fusion | bytes 4202496 | tf_op jit(solution)/shard_map/gather | solution.py:77
  83.2 111.6 %while.26 = (s32[]{:T(128)}, f32[64,64,256]{2,1,0:T(8,128)}, s32[256]{0:T(256)S(1)}, s32[]{:T(128)}, f32[256,4096]{0,1:T(8,128)}, /*index=5*/s32[256]{0:T(256)S(...) while((s32[]{:T(128)}, f32[64,64,256]{2,1,0:T(8,128)}, ...), condition=%wide.region_4.5_spmd, body=%wide.region_2.4_spmd.sunk | while | flops 1613236224 | bytes 69214120 | solution.py:34
  87.0 5.6 %copy.22 = f32[128,64,64]{2,1,0:T(8,128)} copy(f32[128,64,64]{0,2,1:T(8,128)} %bitcast.40) | data formatting | bytes 4194304 | tf_op jit(solution)/shard_map/while/body/eval_jaxpr/reshape | solution.py:30
  92.7 4.3 gather_fusion
  97.0 15.5 %fusion.25 = f32[128,64,256]{2,1,0:T(8,128)} fusion(f32[128,64,64]{2,1,0:T(8,128)} %copy.22, f32[128,64,256]{2,1,0:T(8,128)} %gather_fusion), kind=kOutput, calls=%fused_computation.33.clone.1 | convolution fusion | flops 1610612736 | bytes 18874368 | tf_op jit(solution)/shard_map/while/body/eval_jaxpr/kab,kbf->kaf/dot_general | solution.py:31
  112.5 26.5 %scatter_fusion = f32[64,64,256]{2,1,0:T(8,128)} fusion(f32[64,64,256]{2,1,0:T(8,128)} %get-tuple-element.399, s32[128]{0:T(128)S(1)} %get-tuple-element.376, f32[128,64,256]{2,1,0:T(8,128)} %fusion.25), kind=kCustom, calls=%fused_computation.5.clone.1 | custom fusion | flops 2097152 | bytes 25166336 | tf_op jit(solution)/shard_map/while/body/eval_jaxpr/scatter-add | solution.py:32
  139.6 3.1 dynamic-slice_select_fusion.4
  142.7 5.6 %copy.22 = f32[128,64,64]{2,1,0:T(8,128)} copy(f32[128,64,64]{0,2,1:T(8,128)} %bitcast.40) | data formatting | bytes 4194304 | tf_op jit(solution)/shard_map/while/body/eval_jaxpr/reshape | solution.py:30
  148.4 4.3 gather_fusion
  152.7 15.5 %fusion.25 = f32[128,64,256]{2,1,0:T(8,128)} fusion(f32[128,64,64]{2,1,0:T(8,128)} %copy.22, f32[128,64,256]{2,1,0:T(8,128)} %gather_fusion), kind=kOutput, calls=%fused_computation.33.clone.1 | convolution fusion | flops 1610612736 | bytes 18874368 | tf_op jit(solution)/shard_map/while/body/eval_jaxpr/kab,kbf->kaf/dot_general | solution.py:31
  168.2 26.7 %scatter_fusion = f32[64,64,256]{2,1,0:T(8,128)} fusion(f32[64,64,256]{2,1,0:T(8,128)} %get-tuple-element.399, s32[128]{0:T(128)S(1)} %get-tuple-element.376, f32[128,64,256]{2,1,0:T(8,128)} %fusion.25), kind=kCustom, calls=%fused_computation.5.clone.1 | custom fusion | flops 2097152 | bytes 25166336 | tf_op jit(solution)/shard_map/while/body/eval_jaxpr/scatter-add | solution.py:32
  194.9 73.7 %reduce-scatter.3.cloned.1.call-done = f32[256,256]{1,0:T(8,128)} async-done(((f32[4096,256]{1,0:T(8,128)}), f32[256,256]{1,0:T(8,128)}) %reduce-scatter.3.cloned.1.call-update) | async-done | bytes 262160 | tf_op jit(solution)/shard_map/reduce_scatter | solution.py:93
  274.4 48.1 %all-gather.2.cloned.1.call-done = f32[4096,256]{1,0:T(8,128)} async-done(((f32[256,256]{1,0:T(8,128)}), f32[4096,256]{1,0:T(8,128)}) %all-gather.2.cloned.1.call-update) | async-done | bytes 4194320 | tf_op jit(solution)/shard_map/all_gather | solution.py:99
  322.8 97.1 %while.27 = (s32[]{:T(128)}, f32[32,64,256]{2,1,0:T(8,128)S(1)}, s32[256]{0:T(256)S(1)}, s32[]{:T(128)}, f32[256,4096]{0,1:T(8,128)}, /*index=5*/s32[256]{0:T(25...) while((s32[]{:T(128)}, f32[32,64,256]{2,1,0:T(8,128)S(1)}, ...), condition=%wide.region_8.9_spmd, body=%wide.region_6.8_spmd.sunk | while | flops 1613236224 | bytes 69214120 | solution.py:34
  326.5 5.6 %copy.23 = f32[128,64,64]{1,2,0:T(8,128)} copy(f32[128,64,64]{0,2,1:T(8,128)} %bitcast.41) | data formatting | bytes 4194304 | tf_op jit(solution)/shard_map/while/body/eval_jaxpr/reshape | solution.py:30
  332.2 6.5 %gather_fusion.1 = f32[128,64,256]{2,1,0:T(8,128)} fusion(f32[64,64,256]{2,1,0:T(8,128)} %get-tuple-element.448, s32[1024]{0:T(1024)S(1)} %pad_clamp_fusion.6), kind=kCustom, calls=%fused_computation.1.clone.1 | custom fusion | bytes 16777728 | tf_op jit(solution)/shard_map/while/body/eval_jaxpr/gather | solution.py:31
  338.7 15.5 %fusion.28 = f32[128,64,256]{2,1,0:T(8,128)} fusion(f32[128,64,64]{1,2,0:T(8,128)} %copy.23, f32[128,64,256]{2,1,0:T(8,128)} %gather_fusion.1), kind=kOutput, calls=%fused_computation.34.clone.1 | convolution fusion | flops 1610612736 | bytes 18874368 | tf_op jit(solution)/shard_map/while/body/eval_jaxpr/kba,kbf->kaf/dot_general | solution.py:31
  354.2 17.1 %scatter_fusion.1 = f32[32,64,256]{2,1,0:T(8,128)S(1)} fusion(f32[32,64,256]{2,1,0:T(8,128)S(1)} %get-tuple-element.432, s32[128]{0:T(128)S(1)} %get-tuple-element.385, f32[128,64,256]{2,1,0:T(8,128)} %fusion.28), kind=kCustom, calls=%fused_computation.6.clone.1 | custom fusion | flops 2097152 | bytes 25166336 | tf_op jit(solution)/shard_map/while/body/eval_jaxpr/scatter-add | solution.py:32
  372.0 3.1 dynamic-slice_select_fusion.5
  375.1 5.6 %copy.23 = f32[128,64,64]{1,2,0:T(8,128)} copy(f32[128,64,64]{0,2,1:T(8,128)} %bitcast.41) | data formatting | bytes 4194304 | tf_op jit(solution)/shard_map/while/body/eval_jaxpr/reshape | solution.py:30
  380.8 6.5 %gather_fusion.1 = f32[128,64,256]{2,1,0:T(8,128)} fusion(f32[64,64,256]{2,1,0:T(8,128)} %get-tuple-element.448, s32[1024]{0:T(1024)S(1)} %pad_clamp_fusion.6), kind=kCustom, calls=%fused_computation.1.clone.1 | custom fusion | bytes 16777728 | tf_op jit(solution)/shard_map/while/body/eval_jaxpr/gather | solution.py:31
  387.2 15.5 %fusion.28 = f32[128,64,256]{2,1,0:T(8,128)} fusion(f32[128,64,64]{1,2,0:T(8,128)} %copy.23, f32[128,64,256]{2,1,0:T(8,128)} %gather_fusion.1), kind=kOutput, calls=%fused_computation.34.clone.1 | convolution fusion | flops 1610612736 | bytes 18874368 | tf_op jit(solution)/shard_map/while/body/eval_jaxpr/kba,kbf->kaf/dot_general | solution.py:31
  402.7 17.1 %scatter_fusion.1 = f32[32,64,256]{2,1,0:T(8,128)S(1)} fusion(f32[32,64,256]{2,1,0:T(8,128)S(1)} %get-tuple-element.432, s32[128]{0:T(128)S(1)} %get-tuple-element.385, f32[128,64,256]{2,1,0:T(8,128)} %fusion.28), kind=kCustom, calls=%fused_computation.6.clone.1 | custom fusion | flops 2097152 | bytes 25166336 | tf_op jit(solution)/shard_map/while/body/eval_jaxpr/scatter-add | solution.py:32
  421.2 65.0 %psum.15 = f32[256]{0:T(256)S(1)} all-reduce(f32[256]{0:T(256)S(1)} %get-tuple-element.286), channel_id=1, replica_groups=mesh['row'=16,'col'=8] {'row','col'}, use_global_device_ids=true, to_apply=%region_12.13 | all-reduce | flops 256 | bytes 2048 | tf_op jit(solution)/shard_map/psum | solution.py:117
  488.5 16.8 %reduce-scatter.5.cloned.1.call-done = f32[256,256]{1,0:T(8,128)} async-done(((f32[2048,256]{1,0:T(8,128)}), f32[256,256]{1,0:T(8,128)}) %reduce-scatter.5.cloned.1.call-update) | async-done | bytes 262160 | tf_op jit(solution)/shard_map/reduce_scatter | solution.py:112
  (60 shorter events, 30.0 us)
Async XLA Ops:
  7.2 261.4 %copy-start = (f32[256,256]{1,0:T(8,128)S(1)}, f32[256,256]{1,0:T(8,128)}, u32[]{:S(2)}) copy-start(f32[256,256]{1,0:T(8,128)} %param.19) | copy-start | bytes 786436
  13.8 20.6 %all-to-all-start.1 = ((f32[128,1,16]{2,1,0:T(1,128)}), f32[128,1,16]{2,1,0:T(1,128)S(1)}, u32[]{:S(2)}, u32[]{:S(2)}) async-start(f32[128,1,16]{2,1,0:T(1,128)} %bitcast.9), calls=%async_computation.1 | async-start | bytes 131072 | tf_op jit(solution)/shard_map/all_to_all | solution.py:74
  36.1 35.1 %all-to-all-start = ((f32[128,16,256]{2,1,0:T(8,128)}), f32[128,16,256]{2,1,0:T(8,128)S(1)}, u32[]{:S(2)}, u32[]{:S(2)}) async-start(f32[128,16,256]{2,1,0:T(8,128)} %bitcast.44), calls=%async_computation | async-start | bytes 4194304 | tf_op jit(solution)/shard_map/all_to_all | solution.py:73
  40.7 227.8 %reduce-scatter.3.cloned.1.call-start = ((), (), s32[]{:S(2)}) async-start(), calls=%async_computation.4 | async-start | bytes 4456448 | tf_op jit(solution)/shard_map/reduce_scatter | solution.py:93
  71.1 1.4 copy-start.3
  80.7 2.5 copy-start.4
  80.7 2.5 copy-start.5
  194.8 73.8 %copy-start.6 = (f32[256,256]{1,0:T(8,128)S(1)}, f32[256,256]{1,0:T(8,128)}, u32[]{:S(2)}) copy-start(f32[256,256]{1,0:T(8,128)} %param.21) | copy-start | bytes 786436
  194.8 73.8 %copy-start.7 = (f32[256]{0:T(256)S(1)}, f32[256]{0:T(256)}, u32[]{:S(2)}) copy-start(f32[256]{0:T(256)} %param.20) | copy-start | bytes 3076
  194.8 127.7 %all-gather.2.cloned.1.call-start = ((), (), s32[]{:S(2)}) async-start(), calls=%async_computation.5 | async-start | bytes 4456448 | tf_op jit(solution)/shard_map/all_gather | solution.py:99
  271.8 215.0 %all-reduce.2.cloned.1.call-start = ((), (), s32[]{:S(2)}) async-start(), calls=%async_computation.7 | async-start | bytes 524288 | tf_op jit(solution)/shard_map/psum | solution.py:117
  274.4 230.9 %reduce-scatter.5.cloned.1.call-start = ((), (), s32[]{:S(2)}) async-start(), calls=%async_computation.6 | async-start | bytes 2359296 | tf_op jit(solution)/shard_map/reduce_scatter | solution.py:112
  419.8 1.4 copy-start.2
  419.8 85.5 %copy-start.1 = (f32[256,256]{1,0:T(8,128)S(1)}, f32[256,256]{1,0:T(8,128)}, u32[]{:S(2)}) copy-start(f32[256,256]{1,0:T(8,128)} %param.19) | copy-start | bytes 786436
Sparse Core Ops, SparseCore 0:
  195.0 73.5 reduce-scatter.2
  272.0 50.5 all-gather.1
  327.9 142.9 all-reduce.1
  473.7 31.5 reduce-scatter.4
where the time goes:
time: 514 us; the launch traced here: 512 us
  waiting for transfers between devices  166 us (32%)
  other arithmetic  114 us (22%)
  local copies, waits for them, and re-layouts  69.6 us (14%)
  matrix products  67.5 us (13%)
  blocking collectives  65 us (13%)
  starting transfers between devices  16.2 us (3%)
  between operations  13.9 us (3%)
    scatter-add x4, other arithmetic, one_group(): return partial_sum.at[into_at].add(terms)  87.3 us
    reduce_scatter x1, waiting for transfers between devices, on_device(): lax.psum_scatter(partial_value, 'row', scatter_dimension=0, tiled=True)  73.7 us
    psum x1, blocking collectives, on_device(): grad_w, grad_b = lax.psum((local_w, local_b), ('row', 'col'))  65 us
    dot_general x4, matrix products, one_group(): jnp.einsum(pattern, group_vals, source_blocks[from_at], precision=precise)  62 us
    all_gather x1, waiting for transfers between devices, on_device(): column = lax.all_gather(grad_hidden, 'row', axis=0, tiled=True)  48.1 us
    reshape x4, local copies, waits for them, and re-layouts, one_group(): group_vals = group_vals.reshape(group_size, block_size, block_size)  22.4 us
    gather x4, local copies, waits for them, and re-layouts, one_group(): source_blocks[from_at]  21.6 us
    all_to_all x1, waiting for transfers between devices, on_device(): lax.all_to_all(sent_rows, ('row', 'col'), split_axis=0, concat_axis=0, ti...  19.4 us
  transfers between devices with their start and end apart: 6, of which 5 were waited for; matrix products, arithmetic and copies ran while one was open for 22% of the time, Pallas kernels for 0%

commit v1 on v0

--- a/solution.py
+++ b/solution.py
@@ -96,7 +96,26 @@
     output = preact * squashed
     grad_pre = cotangent * squashed * (1.0 + preact * (1.0 - squashed))
     grad_hidden = jnp.dot(grad_pre, weight.T, precision=precise)
-    column = lax.all_gather(grad_hidden, "row", axis=0, tiled=True)
+    size, index, width = (lax.axis_size("row"), lax.axis_index("row"), grad_hidden.shape[0])
+    ahead = [(i, (i + 1) % size) for i in range(size)]
+    downward = [(i, (i - 1) % size) for i in range(size)]
+    filled = jnp.zeros(
+        (*grad_hidden.shape[:0], size * width, *grad_hidden.shape[0 + 1 :]), grad_hidden.dtype
+    )
+    filled = lax.dynamic_update_slice_in_dim(filled, grad_hidden, index * width, axis=0)
+    from_left = from_right = grad_hidden
+    middle = size // 2
+    for hop in range(1, middle + 1):
+        from_left = lax.ppermute(from_left, "row", ahead)
+        filled = lax.dynamic_update_slice_in_dim(
+            filled, from_left, (index - hop) % size * width, axis=0
+        )
+        if hop < size - middle:
+            from_right = lax.ppermute(from_right, "row", downward)
+            filled = lax.dynamic_update_slice_in_dim(
+                filled, from_right, (index + hop) % size * width, axis=0
+            )
+    column = filled
     partial_x = accumulate(
         jnp.zeros((in_blocks, block_size, feat_width), jnp.float32),
         column.reshape(out_blocks, block_size, feat_width),

time: 514 us -> 538 us (1.047)
  starting transfers between devices: 16.2 us -> 55.2 us
  waiting for transfers between devices: 166 us -> 135 us
  local copies, waits for them, and re-layouts: 69.6 us -> 82.6 us
    all_gather x1 -> x0, waiting for transfers between devices: 48.1 us -> none  [on_device(): column = lax.all_gather(grad_hidden, 'row', axis=0, tiled=True)]
    ppermute x0 -> x15, starting transfers between devices: none -> 39 us  [the longest x7 37.8 us: on_device(): from_right = lax.ppermute(from_right, 'row', downward)]
    ppermute x0 -> x15, waiting for transfers between devices: none -> 34.8 us  [the longest x8 32.8 us: on_device(): from_left = lax.ppermute(from_left, 'row', ahead)]
    reduce_scatter x1, waiting for transfers between devices: 16.8 us -> 0.01 us  [on_device(): lax.psum_scatter(partial_x.reshape(group_rows, feat_width), 'col', scatte...]
    dynamic_update_slice x0 -> x15, local copies, waits for them, and re-layouts: none -> 10.8 us  [the longest x8 5.73 us: on_device(): lax.dynamic_update_slice_in_dim(filled, from_left, (index - hop) % size *...]
  transfers between devices with their start and end apart: 6 -> 20, of which waited for: 5 -> 14; matrix products, arithmetic and copies ran while one was open for 22% -> 23% of each run, Pallas kernels for 0% -> 0%
where the time goes in v1:
time: 538 us; the launch traced here: 531 us
  waiting for transfers between devices  135 us (25%)
  other arithmetic  114 us (21%)
  local copies, waits for them, and re-layouts  82.6 us (15%)
  matrix products  66.7 us (12%)
  blocking collectives  62.6 us (12%)
  starting transfers between devices  55.2 us (10%)
  between operations  14.1 us (3%)
    scatter-add x4, other arithmetic, one_group(): return partial_sum.at[into_at].add(terms)  87.3 us
    reduce_scatter x1, waiting for transfers between devices, on_device(): lax.psum_scatter(partial_value, 'row', scatter_dimension=0, tiled=True)  73.4 us
    psum x1, blocking collectives, on_device(): grad_w, grad_b = lax.psum((local_w, local_b), ('row', 'col'))  62.6 us
    dot_general x4, matrix products, one_group(): jnp.einsum(pattern, group_vals, source_blocks[from_at], precision=precise)  62.1 us
    ppermute x7, starting transfers between devices, on_device(): from_right = lax.ppermute(from_right, 'row', downward)  37.8 us
    ppermute x8, waiting for transfers between devices, on_device(): from_left = lax.ppermute(from_left, 'row', ahead)  32.8 us
    reshape x4, local copies, waits for them, and re-layouts, one_group(): group_vals = group_vals.reshape(group_size, block_size, block_size)  22.5 us
    gather x4, local copies, waits for them, and re-layouts, one_group(): source_blocks[from_at]  21.6 us
  transfers between devices with their start and end apart: 20, of which 14 were waited for; matrix products, arithmetic and copies ran while one was open for 23% of the time, Pallas kernels for 0%

profile of v1, /device:TPU:0, one launch (start us, length us, event | category | flops | bytes accessed | tf_op | source)
XLA Modules:
  0.0 530.8 jit_solution(737384627845460811)
XLA Ops:
  13.8 11.2 %all-to-all-start.1 = ((f32[128,1,16]{2,1,0:T(1,128)}), f32[128,1,16]{2,1,0:T(1,128)S(1)}, u32[]{:S(2)}, u32[]{:S(2)}) async-start(f32[128,1,16]{2,1,0:T(1,128)} %bitcast.9), calls=%async_computation.1 | async-start | bytes 131072 | tf_op jit(solution)/shard_map/all_to_all | solution.py:74
  26.9 7.5 %all-to-all-done.1 = f32[128,1,16]{2,1,0:T(1,128)S(1)} async-done(((f32[128,1,16]{2,1,0:T(1,128)}), f32[128,1,16]{2,1,0:T(1,128)S(1)}, u32[]{:S(2)}, u32[]{:S(2)}) %all-to-all-start.1) | async-done | bytes 8224 | tf_op jit(solution)/shard_map/all_to_all | solution.py:74
  36.1 4.6 all-to-all-start
  40.8 5.6 %copy.19 = f32[1,1,256,4096]{2,3,1,0:T(8,128)} copy(f32[1,1,256,4096]{3,2,1,0:T(8,128)} %param.15) | data formatting | bytes 8388608 | tf_op args[2]
  46.7 5.0 sort.35
  51.7 19.4 %all-to-all-done = f32[128,16,256]{2,1,0:T(8,128)S(1)} async-done(((f32[128,16,256]{2,1,0:T(8,128)}), f32[128,16,256]{2,1,0:T(8,128)S(1)}, u32[]{:S(2)}, u32[]{:S(2)}) %all-to-all-start) | async-done | bytes 2097184 | tf_op jit(solution)/shard_map/all_to_all | solution.py:73
  72.5 8.2 %gather_fusion.4 = f32[2048,256]{1,0:T(8,128)S(1)} fusion(f32[2048,256]{1,0:T(8,128)} %bitcast.41, s32[2048]{0:T(1024)S(1)} %fusion.1), kind=kCustom, calls=%fused_computation.4 | custom fusion | bytes 4202496 | tf_op jit(solution)/shard_map/gather | solution.py:77
  83.2 112.0 %while.26 = (s32[]{:T(128)}, f32[64,64,256]{2,1,0:T(8,128)}, s32[256]{0:T(256)S(1)}, s32[]{:T(128)}, f32[256,4096]{0,1:T(8,128)}, /*index=5*/s32[256]{0:T(256)S(...) while((s32[]{:T(128)}, f32[64,64,256]{2,1,0:T(8,128)}, ...), condition=%wide.region_4.5_spmd, body=%wide.region_2.4_spmd.sunk | while | flops 1613236224 | bytes 69214128 | solution.py:34
  87.4 5.6 %copy.22 = f32[128,64,64]{2,1,0:T(8,128)} copy(f32[128,64,64]{0,2,1:T(8,128)} %bitcast.39) | data formatting | bytes 4194304 | tf_op jit(solution)/shard_map/while/body/eval_jaxpr/reshape | solution.py:30
  97.4 15.5 %fusion.24 = f32[128,64,256]{2,1,0:T(8,128)} fusion(f32[128,64,64]{2,1,0:T(8,128)} %copy.22, f32[128,64,256]{2,1,0:T(8,128)} %gather_fusion), kind=kOutput, calls=%fused_computation.49.clone.1 | convolution fusion | flops 1610612736 | bytes 18874368 | tf_op jit(solution)/shard_map/while/body/eval_jaxpr/kab,kbf->kaf/dot_general | solution.py:31
  112.8 26.6 %scatter_fusion = f32[64,64,256]{2,1,0:T(8,128)} fusion(f32[64,64,256]{2,1,0:T(8,128)} %get-tuple-element.401, s32[128]{0:T(128)S(1)} %get-tuple-element.378, f32[128,64,256]{2,1,0:T(8,128)} %fusion.24), kind=kCustom, calls=%fused_computation.5.clone.1 | custom fusion | flops 2097152 | bytes 25166336 | tf_op jit(solution)/shard_map/while/body/eval_jaxpr/scatter-add | solution.py:32
  143.2 5.6 %copy.22 = f32[128,64,64]{2,1,0:T(8,128)} copy(f32[128,64,64]{0,2,1:T(8,128)} %bitcast.39) | data formatting | bytes 4194304 | tf_op jit(solution)/shard_map/while/body/eval_jaxpr/reshape | solution.py:30
  153.1 15.5 %fusion.24 = f32[128,64,256]{2,1,0:T(8,128)} fusion(f32[128,64,64]{2,1,0:T(8,128)} %copy.22, f32[128,64,256]{2,1,0:T(8,128)} %gather_fusion), kind=kOutput, calls=%fused_computation.49.clone.1 | convolution fusion | flops 1610612736 | bytes 18874368 | tf_op jit(solution)/shard_map/while/body/eval_jaxpr/kab,kbf->kaf/dot_general | solution.py:31
  168.6 26.6 %scatter_fusion = f32[64,64,256]{2,1,0:T(8,128)} fusion(f32[64,64,256]{2,1,0:T(8,128)} %get-tuple-element.401, s32[128]{0:T(128)S(1)} %get-tuple-element.378, f32[128,64,256]{2,1,0:T(8,128)} %fusion.24), kind=kCustom, calls=%fused_computation.5.clone.1 | custom fusion | flops 2097152 | bytes 25166336 | tf_op jit(solution)/shard_map/while/body/eval_jaxpr/scatter-add | solution.py:32
  195.5 73.4 %reduce-scatter.3.cloned.1.call-done = f32[256,256]{1,0:T(8,128)} async-done(((f32[4096,256]{1,0:T(8,128)}), f32[256,256]{1,0:T(8,128)}) %reduce-scatter.3.cloned.1.call-update) | async-done | bytes 262160 | tf_op jit(solution)/shard_map/reduce_scatter | solution.py:93
  284.1 5.3 %collective-permute-start.3 = (f32[256,256]{1,0:T(8,128)S(1)}, f32[256,256]{1,0:T(8,128)S(1)}, u32[]{:S(2)}, u32[]{:S(2)}) collective-permute-start(f32[256,256]{1,0:T(8,128)S(1)} %collective-permute-done.1), channel_id=1, source_target_pairs={{0,120},{8,0},{16,8},{24,16},{32,24},{40,32},{48,40},{56,48},{64,5... | collective-permute-start | bytes 786440 | tf_op jit(solution)/shard_map/ppermute | solution.py:114
  293.8 5.3 %collective-permute-start.5 = (f32[256,256]{1,0:T(8,128)S(1)}, f32[256,256]{1,0:T(8,128)S(1)}, u32[]{:S(2)}, u32[]{:S(2)}) collective-permute-start(f32[256,256]{1,0:T(8,128)S(1)} %collective-permute-done.3), channel_id=1, source_target_pairs={{0,120},{8,0},{16,8},{24,16},{32,24},{40,32},{48,40},{56,48},{64,5... | collective-permute-start | bytes 786440 | tf_op jit(solution)/shard_map/ppermute | solution.py:114
  305.6 5.3 %collective-permute-start.7 = (f32[256,256]{1,0:T(8,128)S(1)}, f32[256,256]{1,0:T(8,128)S(1)}, u32[]{:S(2)}, u32[]{:S(2)}) collective-permute-start(f32[256,256]{1,0:T(8,128)S(1)} %collective-permute-done.5), channel_id=1, source_target_pairs={{0,120},{8,0},{16,8},{24,16},{32,24},{40,32},{48,40},{56,48},{64,5... | collective-permute-start | bytes 786440 | tf_op jit(solution)/shard_map/ppermute | solution.py:114
  315.9 5.8 %collective-permute-start.9 = (f32[256,256]{1,0:T(8,128)S(1)}, f32[256,256]{1,0:T(8,128)S(1)}, u32[]{:S(2)}, u32[]{:S(2)}) collective-permute-start(f32[256,256]{1,0:T(8,128)S(1)} %collective-permute-done.7), channel_id=1, source_target_pairs={{0,120},{8,0},{16,8},{24,16},{32,24},{40,32},{48,40},{56,48},{64,5... | collective-permute-start | bytes 786440 | tf_op jit(solution)/shard_map/ppermute | solution.py:114
  327.8 5.8 %collective-permute-start.11 = (f32[256,256]{1,0:T(8,128)S(1)}, f32[256,256]{1,0:T(8,128)S(1)}, u32[]{:S(2)}, u32[]{:S(2)}) collective-permute-start(f32[256,256]{1,0:T(8,128)S(1)} %collective-permute-done.9), channel_id=1, source_target_pairs={{0,120},{8,0},{16,8},{24,16},{32,24},{40,32},{48,40},{56,48},{64,5... | collective-permute-start | bytes 786440 | tf_op jit(solution)/shard_map/ppermute | solution.py:114
  340.0 5.8 %collective-permute-start.13 = (f32[256,256]{1,0:T(8,128)S(1)}, f32[256,256]{1,0:T(8,128)S(1)}, u32[]{:S(2)}, u32[]{:S(2)}) collective-permute-start(f32[256,256]{1,0:T(8,128)S(1)} %collective-permute-done.11), channel_id=1, source_target_pairs={{0,120},{8,0},{16,8},{24,16},{32,24},{40,32},{48,40},{56,48},{64,5... | collective-permute-start | bytes 786440 | tf_op jit(solution)/shard_map/ppermute | solution.py:114
  352.2 7.6 %collective-permute-done.14 = f32[256,256]{1,0:T(8,128)S(1)} collective-permute-done((f32[256,256]{1,0:T(8,128)S(1)}, f32[256,256]{1,0:T(8,128)S(1)}, u32[]{:S(2)}, u32[]{:S(2)}) %collective-permute-start.14) | collective-permute-done | bytes 262176 | tf_op jit(solution)/shard_map/ppermute | solution.py:109
  360.7 97.2 %while.27 = (s32[]{:T(128)}, f32[32,64,256]{2,1,0:T(8,128)S(1)}, s32[256]{0:T(256)S(1)}, s32[]{:T(128)}, f32[256,4096]{0,1:T(8,128)}, /*index=5*/s32[256]{0:T(25...) while((s32[]{:T(128)}, f32[32,64,256]{2,1,0:T(8,128)S(1)}, ...), condition=%wide.region_8.9_spmd, body=%wide.region_6.8_spmd.sunk | while | flops 1613236224 | bytes 69214128 | solution.py:34
  364.5 5.6 %copy.23 = f32[128,64,64]{1,2,0:T(8,128)} copy(f32[128,64,64]{0,2,1:T(8,128)} %bitcast.40) | data formatting | bytes 4194304 | tf_op jit(solution)/shard_map/while/body/eval_jaxpr/reshape | solution.py:30
  370.2 6.5 %gather_fusion.1 = f32[128,64,256]{2,1,0:T(8,128)} fusion(f32[64,64,256]{2,1,0:T(8,128)} %get-tuple-element.450, s32[1024]{0:T(1024)S(1)} %pad_clamp_fusion.6), kind=kCustom, calls=%fused_computation.1.clone.1 | custom fusion | bytes 16777728 | tf_op jit(solution)/shard_map/while/body/eval_jaxpr/gather | solution.py:31
  376.7 15.5 %fusion.27 = f32[128,64,256]{2,1,0:T(8,128)} fusion(f32[128,64,64]{1,2,0:T(8,128)} %copy.23, f32[128,64,256]{2,1,0:T(8,128)} %gather_fusion.1), kind=kOutput, calls=%fused_computation.50.clone.1 | convolution fusion | flops 1610612736 | bytes 18874368 | tf_op jit(solution)/shard_map/while/body/eval_jaxpr/kba,kbf->kaf/dot_general | solution.py:31
  392.2 17.1 %scatter_fusion.1 = f32[32,64,256]{2,1,0:T(8,128)S(1)} fusion(f32[32,64,256]{2,1,0:T(8,128)S(1)} %get-tuple-element.434, s32[128]{0:T(128)S(1)} %get-tuple-element.387, f32[128,64,256]{2,1,0:T(8,128)} %fusion.27), kind=kCustom, calls=%fused_computation.6.clone.1 | custom fusion | flops 2097152 | bytes 25166336 | tf_op jit(solution)/shard_map/while/body/eval_jaxpr/scatter-add | solution.py:32
  413.1 5.6 %copy.23 = f32[128,64,64]{1,2,0:T(8,128)} copy(f32[128,64,64]{0,2,1:T(8,128)} %bitcast.40) | data formatting | bytes 4194304 | tf_op jit(solution)/shard_map/while/body/eval_jaxpr/reshape | solution.py:30
  418.7 6.5 %gather_fusion.1 = f32[128,64,256]{2,1,0:T(8,128)} fusion(f32[64,64,256]{2,1,0:T(8,128)} %get-tuple-element.450, s32[1024]{0:T(1024)S(1)} %pad_clamp_fusion.6), kind=kCustom, calls=%fused_computation.1.clone.1 | custom fusion | bytes 16777728 | tf_op jit(solution)/shard_map/while/body/eval_jaxpr/gather | solution.py:31
  425.2 15.6 %fusion.27 = f32[128,64,256]{2,1,0:T(8,128)} fusion(f32[128,64,64]{1,2,0:T(8,128)} %copy.23, f32[128,64,256]{2,1,0:T(8,128)} %gather_fusion.1), kind=kOutput, calls=%fused_computation.50.clone.1 | convolution fusion | flops 1610612736 | bytes 18874368 | tf_op jit(solution)/shard_map/while/body/eval_jaxpr/kba,kbf->kaf/dot_general | solution.py:31
  440.8 17.1 %scatter_fusion.1 = f32[32,64,256]{2,1,0:T(8,128)S(1)} fusion(f32[32,64,256]{2,1,0:T(8,128)S(1)} %get-tuple-element.434, s32[128]{0:T(128)S(1)} %get-tuple-element.387, f32[128,64,256]{2,1,0:T(8,128)} %fusion.27), kind=kCustom, calls=%fused_computation.6.clone.1 | custom fusion | flops 2097152 | bytes 25166336 | tf_op jit(solution)/shard_map/while/body/eval_jaxpr/scatter-add | solution.py:32
  459.2 62.6 %psum.15 = f32[256]{0:T(256)S(1)} all-reduce(f32[256]{0:T(256)S(1)} %get-tuple-element.286), channel_id=1, replica_groups=mesh['row'=16,'col'=8] {'row','col'}, use_global_device_ids=true, to_apply=%region_12.13 | all-reduce | flops 256 | bytes 2048 | tf_op jit(solution)/shard_map/psum | solution.py:136
  (105 shorter events, 92.6 us)
Async XLA Ops:
  7.2 261.7 %copy-start = (f32[256,256]{1,0:T(8,128)S(1)}, f32[256,256]{1,0:T(8,128)}, u32[]{:S(2)}) copy-start(f32[256,256]{1,0:T(8,128)} %param.19) | copy-start | bytes 786436
  13.8 20.6 %all-to-all-start.1 = ((f32[128,1,16]{2,1,0:T(1,128)}), f32[128,1,16]{2,1,0:T(1,128)S(1)}, u32[]{:S(2)}, u32[]{:S(2)}) async-start(f32[128,1,16]{2,1,0:T(1,128)} %bitcast.9), calls=%async_computation.1 | async-start | bytes 131072 | tf_op jit(solution)/shard_map/all_to_all | solution.py:74
  36.1 35.1 %all-to-all-start = ((f32[128,16,256]{2,1,0:T(8,128)}), f32[128,16,256]{2,1,0:T(8,128)S(1)}, u32[]{:S(2)}, u32[]{:S(2)}) async-start(f32[128,16,256]{2,1,0:T(8,128)} %bitcast.43), calls=%async_computation | async-start | bytes 4194304 | tf_op jit(solution)/shard_map/all_to_all | solution.py:73
  40.7 228.2 %reduce-scatter.3.cloned.1.call-start = ((), (), s32[]{:S(2)}) async-start(), calls=%async_computation.4 | async-start | bytes 4456448 | tf_op jit(solution)/shard_map/reduce_scatter | solution.py:93
  71.1 1.3 copy-start.3
  80.7 2.5 copy-start.5
  80.7 2.5 copy-start.6
  195.2 73.7 %copy-start.7 = (f32[256,256]{1,0:T(8,128)S(1)}, f32[256,256]{1,0:T(8,128)}, u32[]{:S(2)}) copy-start(f32[256,256]{1,0:T(8,128)} %param.21) | copy-start | bytes 786436
  195.2 73.7 %copy-start.8 = (f32[256]{0:T(256)S(1)}, f32[256]{0:T(256)}, u32[]{:S(2)}) copy-start(f32[256]{0:T(256)} %param.20) | copy-start | bytes 3076
  195.2 327.2 %all-reduce.2.cloned.1.call-start = ((), (), s32[]{:S(2)}) async-start(), calls=%async_computation.6 | async-start | bytes 524288 | tf_op jit(solution)/shard_map/psum | solution.py:136
  268.9 34.6 %copy-start.4 = (f32[256,256]{1,0:T(8,128)S(1)}, f32[256,256]{1,0:T(8,128)}, u32[]{:S(2)}) copy-start(f32[256,256]{1,0:T(8,128)} %reduce-scatter.3.cloned.1.call-done) | copy-start | bytes 786436
  274.4 9.7 %collective-permute-start = (f32[256,256]{1,0:T(8,128)S(1)}, f32[256,256]{1,0:T(8,128)S(1)}, u32[]{:S(2)}, u32[]{:S(2)}) collective-permute-start(f32[256,256]{1,0:T(8,128)S(1)} %get-tuple-element.294), channel_id=1, source_target_pairs={{0,8},{8,16},{16,24},{24,32},{32,40},{40,48},{48,56},{56,64},{64,7... | collective-permute-start | bytes 786440 | tf_op jit(solution)/shard_map/ppermute | solution.py:109
  275.5 8.6 %collective-permute-start.1 = (f32[256,256]{1,0:T(8,128)S(1)}, f32[256,256]{1,0:T(8,128)S(1)}, u32[]{:S(2)}, u32[]{:S(2)}) collective-permute-start(f32[256,256]{1,0:T(8,128)S(1)} %get-tuple-element.294), channel_id=1, source_target_pairs={{0,120},{8,0},{16,8},{24,16},{32,24},{40,32},{48,40},{56,48},{64,5... | collective-permute-start | bytes 786440 | tf_op jit(solution)/shard_map/ppermute | solution.py:114
  284.1 9.7 %collective-permute-start.2 = (f32[256,256]{1,0:T(8,128)S(1)}, f32[256,256]{1,0:T(8,128)S(1)}, u32[]{:S(2)}, u32[]{:S(2)}) collective-permute-start(f32[256,256]{1,0:T(8,128)S(1)} %collective-permute-done), channel_id=1, source_target_pairs={{0,8},{8,16},{16,24},{24,32},{32,40},{40,48},{48,56},{56,64},{64,7... | collective-permute-start | bytes 786440 | tf_op jit(solution)/shard_map/ppermute | solution.py:109
  284.1 9.7 %collective-permute-start.3 = (f32[256,256]{1,0:T(8,128)S(1)}, f32[256,256]{1,0:T(8,128)S(1)}, u32[]{:S(2)}, u32[]{:S(2)}) collective-permute-start(f32[256,256]{1,0:T(8,128)S(1)} %collective-permute-done.1), channel_id=1, source_target_pairs={{0,120},{8,0},{16,8},{24,16},{32,24},{40,32},{48,40},{56,48},{64,5... | collective-permute-start | bytes 786440 | tf_op jit(solution)/shard_map/ppermute | solution.py:114
  293.8 9.7 %collective-permute-start.4 = (f32[256,256]{1,0:T(8,128)S(1)}, f32[256,256]{1,0:T(8,128)S(1)}, u32[]{:S(2)}, u32[]{:S(2)}) collective-permute-start(f32[256,256]{1,0:T(8,128)S(1)} %collective-permute-done.2), channel_id=1, source_target_pairs={{0,8},{8,16},{16,24},{24,32},{32,40},{40,48},{48,56},{56,64},{64,7... | collective-permute-start | bytes 786440 | tf_op jit(solution)/shard_map/ppermute | solution.py:109
  293.8 11.8 %collective-permute-start.5 = (f32[256,256]{1,0:T(8,128)S(1)}, f32[256,256]{1,0:T(8,128)S(1)}, u32[]{:S(2)}, u32[]{:S(2)}) collective-permute-start(f32[256,256]{1,0:T(8,128)S(1)} %collective-permute-done.3), channel_id=1, source_target_pairs={{0,120},{8,0},{16,8},{24,16},{32,24},{40,32},{48,40},{56,48},{64,5... | collective-permute-start | bytes 786440 | tf_op jit(solution)/shard_map/ppermute | solution.py:114
  303.5 10.3 %collective-permute-start.6 = (f32[256,256]{1,0:T(8,128)S(1)}, f32[256,256]{1,0:T(8,128)S(1)}, u32[]{:S(2)}, u32[]{:S(2)}) collective-permute-start(f32[256,256]{1,0:T(8,128)S(1)} %collective-permute-done.4), channel_id=1, source_target_pairs={{0,8},{8,16},{16,24},{24,32},{32,40},{40,48},{48,56},{56,64},{64,7... | collective-permute-start | bytes 786440 | tf_op jit(solution)/shard_map/ppermute | solution.py:109
  304.9 219.2 %reduce-scatter.5.cloned.1.call-start = ((), (), s32[]{:S(2)}) async-start(), calls=%async_computation.5 | async-start | bytes 2359296 | tf_op jit(solution)/shard_map/reduce_scatter | solution.py:131
  305.6 10.2 %collective-permute-start.7 = (f32[256,256]{1,0:T(8,128)S(1)}, f32[256,256]{1,0:T(8,128)S(1)}, u32[]{:S(2)}, u32[]{:S(2)}) collective-permute-start(f32[256,256]{1,0:T(8,128)S(1)} %collective-permute-done.5), channel_id=1, source_target_pairs={{0,120},{8,0},{16,8},{24,16},{32,24},{40,32},{48,40},{56,48},{64,5... | collective-permute-start | bytes 786440 | tf_op jit(solution)/shard_map/ppermute | solution.py:114
  313.9 11.6 %collective-permute-start.8 = (f32[256,256]{1,0:T(8,128)S(1)}, f32[256,256]{1,0:T(8,128)S(1)}, u32[]{:S(2)}, u32[]{:S(2)}) collective-permute-start(f32[256,256]{1,0:T(8,128)S(1)} %collective-permute-done.6), channel_id=1, source_target_pairs={{0,8},{8,16},{16,24},{24,32},{32,40},{40,48},{48,56},{56,64},{64,7... | collective-permute-start | bytes 786440 | tf_op jit(solution)/shard_map/ppermute | solution.py:109
  315.9 11.9 %collective-permute-start.9 = (f32[256,256]{1,0:T(8,128)S(1)}, f32[256,256]{1,0:T(8,128)S(1)}, u32[]{:S(2)}, u32[]{:S(2)}) collective-permute-start(f32[256,256]{1,0:T(8,128)S(1)} %collective-permute-done.7), channel_id=1, source_target_pairs={{0,120},{8,0},{16,8},{24,16},{32,24},{40,32},{48,40},{56,48},{64,5... | collective-permute-start | bytes 786440 | tf_op jit(solution)/shard_map/ppermute | solution.py:114
  325.5 12.6 %collective-permute-start.10 = (f32[256,256]{1,0:T(8,128)S(1)}, f32[256,256]{1,0:T(8,128)S(1)}, u32[]{:S(2)}, u32[]{:S(2)}) collective-permute-start(f32[256,256]{1,0:T(8,128)S(1)} %collective-permute-done.8), channel_id=1, source_target_pairs={{0,8},{8,16},{16,24},{24,32},{32,40},{40,48},{48,56},{56,64},{64,7... | collective-permute-start | bytes 786440 | tf_op jit(solution)/shard_map/ppermute | solution.py:109
  327.8 12.2 %collective-permute-start.11 = (f32[256,256]{1,0:T(8,128)S(1)}, f32[256,256]{1,0:T(8,128)S(1)}, u32[]{:S(2)}, u32[]{:S(2)}) collective-permute-start(f32[256,256]{1,0:T(8,128)S(1)} %collective-permute-done.9), channel_id=1, source_target_pairs={{0,120},{8,0},{16,8},{24,16},{32,24},{40,32},{48,40},{56,48},{64,5... | collective-permute-start | bytes 786440 | tf_op jit(solution)/shard_map/ppermute | solution.py:114
  338.0 11.7 %collective-permute-start.12 = (f32[256,256]{1,0:T(8,128)S(1)}, f32[256,256]{1,0:T(8,128)S(1)}, u32[]{:S(2)}, u32[]{:S(2)}) collective-permute-start(f32[256,256]{1,0:T(8,128)S(1)} %collective-permute-done.10), channel_id=1, source_target_pairs={{0,8},{8,16},{16,24},{24,32},{32,40},{40,48},{48,56},{56,64},{64,7... | collective-permute-start | bytes 786440 | tf_op jit(solution)/shard_map/ppermute | solution.py:109
  340.0 11.5 %collective-permute-start.13 = (f32[256,256]{1,0:T(8,128)S(1)}, f32[256,256]{1,0:T(8,128)S(1)}, u32[]{:S(2)}, u32[]{:S(2)}) collective-permute-start(f32[256,256]{1,0:T(8,128)S(1)} %collective-permute-done.11), channel_id=1, source_target_pairs={{0,120},{8,0},{16,8},{24,16},{32,24},{40,32},{48,40},{56,48},{64,5... | collective-permute-start | bytes 786440 | tf_op jit(solution)/shard_map/ppermute | solution.py:114
  349.8 10.0 %collective-permute-start.14 = (f32[256,256]{1,0:T(8,128)S(1)}, f32[256,256]{1,0:T(8,128)S(1)}, u32[]{:S(2)}, u32[]{:S(2)}) collective-permute-start(f32[256,256]{1,0:T(8,128)S(1)} %collective-permute-done.12), channel_id=1, source_target_pairs={{0,8},{8,16},{16,24},{24,32},{32,40},{40,48},{48,56},{56,64},{64,7... | collective-permute-start | bytes 786440 | tf_op jit(solution)/shard_map/ppermute | solution.py:109
  457.9 1.3 copy-start.2
  457.9 66.2 %copy-start.1 = (f32[256,256]{1,0:T(8,128)S(1)}, f32[256,256]{1,0:T(8,128)}, u32[]{:S(2)}) copy-start(f32[256,256]{1,0:T(8,128)} %param.19) | copy-start | bytes 786436
Sparse Core Ops, SparseCore 0:
  195.4 73.4 reduce-scatter.2
  305.0 145.7 all-reduce.1
  459.4 30.5 reduce-scatter.4
